TPU v7x, 256 devices: a whole 4x4x8 slice. The times are simulated.
256 devices in a mesh: layer: 8 (over z_hi, y), row: 32 (over x, z_lo, core).
Axes of the slice: x: 4, y: 4, z: 8 (z_hi: 2, z_lo: 4; z = z_hi * 4 + z_lo), core: 2. Of those that a mesh axis runs over, the one named last changes fastest.
Arguments:
- query_grads: bfloat16 [16, 1024, 4096], P('layer', 'row'), may hold values from -6 to 6
- train_grads: bfloat16 [16, 16384, 4096], P('layer', 'row'), may hold values from -0.023925781 to 0.023925781
- left_inverse: float32 [16, 64, 64], P('layer'), may hold values from -0.75 to 0.75
- right_inverse: float32 [16, 64, 64], P('layer'), may hold values from -0.75 to 0.75
Outputs:
- scores: float32 [1024, 16384], P('layer', 'row')
All inputs are finite; a program needn't handle non-finite values.
Results may differ from a plain program's by a relative error of at most 0.0029.
Values may be sent and summed in bfloat16 or wider, within the bound.
A program may use at most 128 MiB of HBM per device.

v0:
```python
import jax
import jax.numpy as jnp
from jax import lax
from jax.sharding import PartitionSpec as P


def on_device(query_grads, train_grads, left_inverse, right_inverse):
    layers, rows, feat = query_grads.shape
    proj = left_inverse.shape[1]
    square = query_grads.astype(jnp.float32).reshape(layers, rows, proj, proj)
    rotated = jnp.einsum(
        "lab,lqbc,lcd->lqad", left_inverse, square, right_inverse, precision=lax.Precision.HIGHEST
    )
    rotated = rotated.reshape(layers, rows, feat).astype(jnp.bfloat16)
    partial_value = jnp.einsum(
        "lqf,ltf->qt",
        lax.all_gather(rotated, "row", axis=1, tiled=True),
        train_grads,
        preferred_element_type=jnp.float32,
    )
    summed = lax.psum(partial_value, "layer")
    block = summed.shape[0] // lax.axis_size("layer")
    return lax.dynamic_slice_in_dim(summed, lax.axis_index("layer") * block, block, 0)


def solution(mesh):
    placed = (
        P("layer", "row", None),
        P("layer", "row", None),
        P("layer", None, None),
        P("layer", None, None),
    )
    return jax.shard_map(
        on_device, mesh=mesh, in_specs=placed, out_specs=P("layer", "row"), check_vma=False
    )
```

profile of v0, /device:TPU:24, one launch (start us, length us, event | category | flops | bytes accessed | tf_op | source)
XLA Modules:
  0.0 275.1 jit_solution(14499633773549307910)
XLA Ops:
  6.5 0.0 copy-start
  6.5 0.0 copy-start.1
  6.5 0.0 all-gather.2.cloned.1.call-start
  6.5 2.1 reshape.5
  8.6 0.0 copy-done
  8.6 1.0 fusion.1
  9.6 0.0 copy-done.1
  9.6 1.9 convolution_convert_fusion
  11.5 1.6 convert_element_type.8
  13.2 0.0 all-gather.2.cloned.1.call-update
  13.2 0.0 all-reduce.2.cloned.1.call-start
  13.2 102.5 %all-gather.2.cloned.1.call-done = bf16[2,1024,4096]{2,1,0:T(8,128)(2,1)} async-done(((bf16[2,32,4096]{2,1,0:T(8,128)(2,1)}), bf16[2,1024,4096]{2,1,0:T(8,128)(2,1)}) %all-gather.2.cloned.1.call-update) | async-done | bytes 16777232 | tf_op jit(solution)/shard_map/all_gather | solution.py:17
  115.7 15.8 %convolution_bitcast_fusion = f32[1024,512]{1,0:T(8,128)} fusion(bf16[2,1024,4096]{2,1,0:T(8,128)(2,1)} %all-gather.2.cloned.1.call-done, bf16[2,512,4096]{2,1,0:T(8,128)(2,1)} %param.5), kind=kOutput, calls=%fused_computation | convolution fusion | flops 8589934592 | bytes 27262976 | tf_op jit(solution)/shard_map/lqf,ltf->qt/dot_general | solution.py:15
  131.6 0.0 all-reduce.2.cloned.1.call-update
  131.6 135.0 %all-reduce.2.cloned.1.call-done = f32[1024,512]{1,0:T(8,128)} async-done(((f32[1024,512]{1,0:T(8,128)}), f32[1024,512]{1,0:T(8,128)}) %all-reduce.2.cloned.1.call-update) | async-done | bytes 2097168 | tf_op jit(solution)/shard_map/psum | solution.py:21
  266.6 1.7 constant_dynamic-slice_fusion
Async XLA Ops:
  6.5 2.1 copy-start
  6.5 3.1 %copy-start.1 = (f32[2,64,64]{2,1,0:T(8,128)S(1)}, f32[2,64,64]{2,1,0:T(8,128)}, u32[]{:S(2)}) copy-start(f32[2,64,64]{2,1,0:T(8,128)} %param.7) | copy-start | bytes 98308
  6.5 109.2 %all-gather.2.cloned.1.call-start = ((), (), s32[]{:S(2)}) async-start(), calls=%async_computation | async-start | bytes 17301504 | tf_op jit(solution)/shard_map/all_gather | solution.py:17
  13.2 253.4 %all-reduce.2.cloned.1.call-start = ((), (), s32[]{:S(2)}) async-start(), calls=%async_computation.1 | async-start | bytes 4194304 | tf_op jit(solution)/shard_map/psum | solution.py:21
Sparse Core Ops, SparseCore 0:
  13.3 102.3 all-gather.1
  131.7 134.8 all-reduce.1
where the time goes:
time: 275 us
  waiting for transfers between devices  238 us (87%)
  matrix products  18.7 us (7%)
  between operations  13.4 us (5%)
  local copies, waits for them, and re-layouts  5.38 us (2%)
    psum x1, waiting for transfers between devices, on_device(): summed = lax.psum(partial_value, 'layer')  135 us
    all_gather x1, waiting for transfers between devices, on_device(): lax.all_gather(rotated, 'row', axis=1, tiled=True)  102 us
    dot_general x1, matrix products, on_device(): jnp.einsum('lqf,ltf->qt', lax.all_gather(rotated, 'row', axis=1, tiled=Tr...  15.8 us
  transfers between devices with their start and end apart: 2, of which 2 were waited for; matrix products, arithmetic and copies ran while one was open for 0% of the time, Pallas kernels for 0%

commit v1 on v0

v1 whole, which is shorter than its diff:
```python
import jax
import jax.numpy as jnp
from jax import lax
from jax.experimental import pallas as pl
from jax.experimental.pallas import tpu as pltpu
from jax.sharding import PartitionSpec as P

MESH = pl.DeviceIdType.MESH
NX, NZ, NG, PIECES = 4, 4, 8, 4
STEPS = NZ * PIECES


def kernel(pre_ref, train_ref, out_ref, held, train, acc, own, stage, landed,
           pre_sem, train_sem, zs, zr, zs2, xs, xr, hs, hr, ps, pr, ss, sr):
    g = lax.axis_index("layer")
    row = lax.axis_index("row")
    core = lax.rem(row, 2)
    z = lax.rem(row // 2, NZ)
    x = row // (2 * NZ)
    upper = z // 2
    end = jnp.where(upper == 1, 3 - z, z) == 0
    zl = jnp.where(upper == 1, 3 - z, z)

    def device(xx, zz, cc):
        return (g, (xx * NZ + zz) * 2 + cc)

    right, left = lax.rem(x + 1, NX), lax.rem(x + NX - 1, NX)
    side = z + 1 - 2 * lax.rem(z, 2)
    across = 3 - z

    def held_z(k):
        c = jnp.where(k == 0, zl, jnp.where(k == 1, 1 - zl, k))
        return jnp.where(upper == 1, 3 - c, c)

    half = pre_ref.shape[2] // 2
    rows = pre_ref.shape[1]
    low, high = pl.ds(0, rows // 2), pl.ds(rows // 2, rows // 2)

    def pre_copy(p):
        return pltpu.make_async_copy(
            pre_ref.at[p // 2, :, pl.ds((p % 2) * half, half)],
            held.at[z, p, core, x], pre_sem.at[p])

    def train_copy(p):
        return pltpu.make_async_copy(
            train_ref.at[p // 2, :, pl.ds((p % 2) * half, half)],
            train.at[p], train_sem.at[p])

    for p in range(PIECES):
        pre_copy(p).start()
    for p in range(PIECES):
        train_copy(p).start()

    barrier = pltpu.get_barrier_semaphore()

    def greet(target):
        pl.semaphore_signal(barrier, inc=1, device_id=target, device_id_type=MESH)

    greet(device(right, z, core))
    greet(device(left, z, core))
    greet(device(x, z, 1 - core))
    greet(device(x, side, core))
    for j in range(1, NG):
        greet((lax.rem(g + j, NG), row))

    greet(device(x, across, core))
    pl.semaphore_wait(barrier, 5 + NG - 1)

    def remote(ref, send_sem, recv_sem, target):
        return pltpu.make_async_remote_copy(
            src_ref=ref, dst_ref=ref, send_sem=send_sem, recv_sem=recv_sem,
            device_id=target, device_id_type=MESH)

    def to_side(k, k_there, p):
        return remote(held.at[held_z(k), p, core, x], zs.at[k_there, p], zr.at[k_there, p], device(x, side, core))

    def to_across(k, k_there, p):
        return remote(held.at[held_z(k), p, core, x], zs2.at[k_there, p], zr.at[k_there, p], device(x, across, core))

    def to_x(k, p, d):
        return remote(held.at[held_z(k), p, core, x], xs.at[d, k, p], xr.at[d, k, p],
                      device(right if d == 0 else left, z, core))

    def from_x(k, p, d):
        return remote(held.at[held_z(k), p, core, left if d == 0 else right], xs.at[d, k, p], xr.at[d, k, p],
                      device(right if d == 0 else left, z, core))

    def relay(k, p, d):
        return remote(held.at[held_z(k), p, core, left if d == 0 else right, low if d == 0 else high],
                      hs.at[d, k, p], hr.at[d, k, p], device(right if d == 0 else left, z, core))

    def to_partner(k, p):
        return remote(held.at[held_z(k), p, core], ps.at[k, p], pr.at[k, p], device(x, z, 1 - core))

    def to_owner(k, xx):
        zz = held_z(k)
        owner = 2 * xx + zz // 2
        return pltpu.make_async_remote_copy(
            src_ref=stage.at[k, xx], dst_ref=landed.at[g, lax.rem(zz, 2)],
            send_sem=ss.at[k, xx], recv_sem=sr.at[g, lax.rem(zz, 2)],
            device_id=(owner, row), device_id_type=MESH)

    inner = jnp.logical_not(end)

    for p in range(PIECES):
        pre_copy(p).wait()
        to_side(0, 1, p).start()

        @pl.when(inner)
        def _():
            to_across(0, 2, p).start()

    def part_z(i):
        early = i - 2
        late = i - 4

        @pl.when(jnp.logical_and(inner, jnp.logical_and(early >= 0, early < PIECES)))
        def _():
            to_side(1, 1, early).wait_recv()
            to_across(1, 3, early).start()
            to_across(2, 2, early).wait_recv()
            to_side(2, 2, early).start()

        @pl.when(jnp.logical_and(inner, jnp.logical_and(late >= 0, late < PIECES)))
        def _():
            to_across(3, 3, late).wait_recv()
            to_side(3, 3, late).start()

    def step(i, carry):
        part_z(i)

        @pl.when(i < STEPS)
        def _():
            k, p = i // PIECES, lax.rem(i, PIECES)

            @pl.when(jnp.logical_and(end, k > 0))
            def _():
                to_side(k, k, p).wait_recv()

            to_x(k, p, 0).start()
            to_x(k, p, 1).start()

        @pl.when(jnp.logical_and(i >= 1, i < STEPS + 1))
        def _():
            s = i - 1
            k, p = s // PIECES, lax.rem(s, PIECES)
            from_x(k, p, 0).wait_recv()
            relay(k, p, 0).start()
            from_x(k, p, 1).wait_recv()
            relay(k, p, 1).start()

        @pl.when(jnp.logical_and(i >= 2, i < STEPS + 2))
        def _():
            s = i - 2
            k, p = s // PIECES, lax.rem(s, PIECES)
            relay(k, p, 0).wait_recv()
            relay(k, p, 1).wait_recv()
            to_partner(k, p).start()

        @pl.when(i >= 3)
        def _():
            s = i - 3
            k, p = s // PIECES, lax.rem(s, PIECES)

            @pl.when(k == 0)
            def _():
                train_copy_dyn(p).wait()

            to_partner(k, p).wait_recv()
            block = held[held_z(k), p].reshape(2 * NX * rows, half)
            term = lax.dot_general(block, train[p], (((1,), (1,)), ((), ())),
                                   preferred_element_type=jnp.float32)

            @pl.when(p == 0)
            def _():
                acc[...] = term

            @pl.when(p > 0)
            def _():
                acc[...] += term

            @pl.when(p == PIECES - 1)
            def _():
                zz = held_z(k)
                for xx in range(NX):
                    mine = (2 * xx + zz // 2) == g

                    @pl.when(mine)
                    def _():
                        for c in range(2):
                            own[lax.rem(zz, 2), pl.ds(c * rows, rows), :] = acc[pl.ds((c * NX + xx) * rows, rows), :]

                    @pl.when(jnp.logical_not(mine))
                    def _():
                        for c in range(2):
                            stage[k, xx, pl.ds(c * rows, rows), :] = acc[
                                pl.ds((c * NX + xx) * rows, rows), :].astype(jnp.bfloat16)
                        to_owner(k, xx).start()

        return carry

    def train_copy_dyn(p):
        return pltpu.make_async_copy(train.at[p], train.at[p], train_sem.at[p])

    lax.fori_loop(0, STEPS + 3, step, 0)

    out_ref[...] = own[...].reshape(out_ref.shape)
    for j in range(1, NG):
        src = lax.rem(g + j, NG)
        for b in range(2):
            pltpu.make_async_remote_copy(
                src_ref=stage.at[0, 0], dst_ref=landed.at[src, b], send_sem=ss.at[0, 0], recv_sem=sr.at[src, b],
                device_id=(src, row), device_id_type=MESH).wait_recv()
        out_ref[...] += landed[src].astype(jnp.float32).reshape(out_ref.shape)

    def drain(s, carry):
        k, p = s // PIECES, lax.rem(s, PIECES)
        for d in range(2):
            to_x(k, p, d).wait_send()
            relay(k, p, d).wait_send()
        to_partner(k, p).wait_send()

        @pl.when(k == 0)
        def _():
            to_side(0, 1, p).wait_send()

        @pl.when(inner)
        def _():
            @pl.when(k == 0)
            def _():
                to_across(0, 2, p).wait_send()

            @pl.when(k == 1)
            def _():
                to_across(1, 3, p).wait_send()

            @pl.when(k >= 2)
            def _():
                to_side(k, k, p).wait_send()

        return carry

    lax.fori_loop(0, STEPS, drain, 0)
    for k in range(NZ):
        for xx in range(NX):
            @pl.when((2 * xx + held_z(k) // 2) != g)
            def _():
                to_owner(k, xx).wait_send()


def scores_of(pre, train_grads):
    layers, rows, feat = pre.shape
    train_rows = train_grads.shape[1]
    half = feat // 2
    queries = NX * NZ * 2 * rows
    block = queries // NG
    dma = pltpu.SemaphoreType.DMA
    return pl.pallas_call(
        kernel,
        out_shape=jax.ShapeDtypeStruct((block, train_rows), jnp.float32),
        in_specs=[pl.BlockSpec(memory_space=pl.ANY)] * 2,
        out_specs=pl.BlockSpec(memory_space=pltpu.VMEM),
        scratch_shapes=[
            pltpu.VMEM((NZ, PIECES, 2, NX, rows, half), jnp.bfloat16),
            pltpu.VMEM((PIECES, train_rows, half), jnp.bfloat16),
            pltpu.VMEM((2 * NX * rows, train_rows), jnp.float32),
            pltpu.VMEM((2, 2 * rows, train_rows), jnp.float32),
            pltpu.VMEM((NZ, NX, 2 * rows, train_rows), jnp.bfloat16),
            pltpu.VMEM((NG, 2, 2 * rows, train_rows), jnp.bfloat16),
            dma((PIECES,)), dma((PIECES,)),
            dma((NZ, PIECES)), dma((NZ, PIECES)), dma((NZ, PIECES)),
            dma((2, NZ, PIECES)), dma((2, NZ, PIECES)),
            dma((2, NZ, PIECES)), dma((2, NZ, PIECES)),
            dma((NZ, PIECES)), dma((NZ, PIECES)),
            dma((NZ, NX)), dma((NG, 2)),
        ],
        compiler_params=pltpu.CompilerParams(
            collective_id=0, has_side_effects=True, vmem_limit_bytes=60 * 1024 * 1024),
    )(pre, train_grads)


def on_device(query_grads, train_grads, left_inverse, right_inverse):
    layers, rows, feat = query_grads.shape
    proj = left_inverse.shape[1]
    square = query_grads.astype(jnp.float32).reshape(layers, rows, proj, proj)
    rotated = jnp.einsum(
        "lab,lqbc,lcd->lqad", left_inverse, square, right_inverse, precision=lax.Precision.HIGHEST
    )
    rotated = rotated.reshape(layers, rows, feat).astype(jnp.bfloat16)
    return scores_of(rotated, train_grads)


def solution(mesh):
    placed = (
        P("layer", "row", None),
        P("layer", "row", None),
        P("layer", None, None),
        P("layer", None, None),
    )
    return jax.shard_map(
        on_device, mesh=mesh, in_specs=placed, out_specs=P("layer", "row"), check_vma=False
    )
```

time: 275 us -> 104 us (0.38)
  waiting for transfers between devices: 238 us -> 0 us
  Pallas kernels: 0 us -> 94.1 us
  matrix products: 18.7 us -> 2.87 us
  between operations: 13.4 us -> 0.05 us
    psum x1 -> x0, waiting for transfers between devices: 135 us -> none  [on_device(): summed = lax.psum(partial_value, 'layer')]
    all_gather x1 -> x0, waiting for transfers between devices: 102 us -> none  [on_device(): lax.all_gather(rotated, 'row', axis=1, tiled=True)]
    pallas_call x0 -> x1, Pallas kernels: none -> 94.1 us  [scores_of(): pl.pallas_call(kernel, out_shape=jax.ShapeDtypeStruct((block, train_rows)...]
    dot_general x1 -> x0, matrix products: 15.8 us -> none  [on_device(): jnp.einsum('lqf,ltf->qt', lax.all_gather(rotated, 'row', axis=1, tiled=Tr...]
  transfers between devices with their start and end apart: 2 -> 0, of which waited for: 2 -> 0; matrix products, arithmetic and copies ran while one was open for 0% -> 0% of each run, Pallas kernels for 0% -> 0%
where the time goes in v1:
time: 104 us; the launch traced here: 102 us
  Pallas kernels  94.1 us (90%)
  local copies, waits for them, and re-layouts  5.37 us (5%)
  matrix products  2.87 us (3%)
    pallas_call x1, Pallas kernels, scores_of(): pl.pallas_call(kernel, out_shape=jax.ShapeDtypeStruct((block, train_rows)...  94.1 us
    dot_general x2, matrix products, on_device(): jnp.einsum('lab,lqbc,lcd->lqad', left_inverse, square, right_inverse, pre...  2.87 us
    reshape x1, local copies, waits for them, and re-layouts, on_device(): square = query_grads.astype(jnp.float32).reshape(layers, rows, proj, proj)  2.09 us

profile of v1, /device:TPU:24, one launch (start us, length us, event | category | flops | bytes accessed | tf_op | source)
XLA Modules:
  0.0 102.4 jit_solution(13342273242302349406)
XLA Ops:
  0.0 0.0 copy-start
  0.0 0.0 copy-start.1
  0.0 2.1 %reshape.5 = bf16[2,32,64,64]{3,2,1,0:T(8,128)(2,1)S(1)} reshape(bf16[2,32,4096]{2,1,0:T(8,128)(2,1)} %param.4) | data formatting | bytes 1048576 | tf_op jit(solution)/shard_map/reshape | solution.py:285
  2.1 0.0 copy-done
  2.1 1.0 fusion.1
  3.1 0.0 copy-done.1
  3.1 1.9 %convolution_convert_fusion = bf16[2,32,64,64]{3,2,1,0:T(8,128)(2,1)S(1)} fusion(f32[2,32,64,64]{2,3,1,0:T(8,128)S(1)} %fusion.1, f32[2,64,64]{2,1,0:T(8,128)S(1)} %copy-done.1), kind=kOutput, calls=%fused_computation | convolution fusion | flops 201588736 | bytes 1605632 | tf_op jit(solution)/shard_map/lab,lqbc,lcd->lqad/dot_general | solution.py:286
  5.0 1.6 %convert_element_type.7.pre_ref = bf16[2,32,4096]{2,1,0:T(8,128)(2,1)} reshape(bf16[2,32,64,64]{3,2,1,0:T(8,128)(2,1)S(1)} %convolution_convert_fusion) | data formatting | bytes 1048576 | tf_op jit(solution)/shard_map/convert_element_type | solution.py:289
  6.6 94.1 %shard_map.46 = f32[128,512]{1,0:T(8,128)} custom-call(bf16[2,32,4096]{2,1,0:T(8,128)(2,1)} %convert_element_type.7.pre_ref, bf16[2,512,4096]{2,1,0:T(8,128)(2,1)} %train_ref.1), custom_call_target="tpu_custom_call" | custom-call | tf_op jit(solution)/shard_map/pallas_call | solution.py:258
  100.7 1.7 %copy.8 = f32[128,512]{1,0:T(8,128)} copy(f32[128,512]{1,0:T(8,128)} %shard_map.46) | data formatting | bytes 524288
Async XLA Ops:
  0.0 2.1 %copy-start = (f32[2,64,64]{2,1,0:T(8,128)S(1)}, f32[2,64,64]{2,1,0:T(8,128)}, u32[]{:S(2)}) copy-start(f32[2,64,64]{2,1,0:T(8,128)} %param.6) | copy-start | bytes 98308
  0.0 3.1 %copy-start.1 = (f32[2,64,64]{2,1,0:T(8,128)S(1)}, f32[2,64,64]{2,1,0:T(8,128)}, u32[]{:S(2)}) copy-start(f32[2,64,64]{2,1,0:T(8,128)} %param.7) | copy-start | bytes 98308

commit v2 on v1

v2 whole, which is shorter than its diff:
```python
import jax
import jax.numpy as jnp
from jax import lax
from jax.experimental import pallas as pl
from jax.experimental.pallas import tpu as pltpu
from jax.sharding import PartitionSpec as P

MESH = pl.DeviceIdType.MESH
NX, NY, NZ, NG = 4, 4, 4, 8
PIECES = 4
STEPS = NZ * PIECES
XPIECES = 2
XCOLS = 768


def kernel(pre_ref, train_ref, out_ref, held, heldx, train, trainx, acc, mine, stage_y, landed_y, stage_z, landed_z,
           stage_d, landed_d, pre_sem, prex_sem, train_sem, trainx_sem, zs, zs2, zr, xs, xr, hs, hr, ps, pr,
           bs, bs2, br, axs, axr, ahs, ahr, aps, apr, ys, yr, ws, wr, ds, dr):
    g = lax.axis_index("layer")
    row = lax.axis_index("row")
    core = lax.rem(row, 2)
    z = lax.rem(row // 2, NZ)
    x = row // (2 * NZ)
    y = lax.rem(g, NY)
    zh = g // NY
    upper = z // 2
    zl = jnp.where(upper == 1, 3 - z, z)
    end = zl == 0
    inner = jnp.logical_not(end)
    right, left = lax.rem(x + 1, NX), lax.rem(x + NX - 1, NX)
    side = z + 1 - 2 * lax.rem(z, 2)
    across = 3 - z
    rows = pre_ref.shape[1]
    feat = pre_ref.shape[2]
    cols = held.shape[-1]
    low, high = pl.ds(0, rows // 2), pl.ds(rows // 2, rows // 2)

    def device(xx, zz, cc):
        return (g, (xx * NZ + zz) * 2 + cc)

    def held_z(k):
        c = jnp.where(k == 0, zl, jnp.where(k == 1, 1 - zl, k))
        return jnp.where(upper == 1, 3 - c, c)

    def pre_copy(p):
        return pltpu.make_async_copy(
            pre_ref.at[p // 2, :, pl.ds((p % 2) * cols, cols)], held.at[z, p, core, x], pre_sem.at[p])

    def prex_copy(q):
        return pltpu.make_async_copy(
            pre_ref.at[q, :, pl.ds(feat - XCOLS, XCOLS)], heldx.at[z, q, core, x], prex_sem.at[q])

    def train_copy(p):
        return pltpu.make_async_copy(
            train_ref.at[p // 2, :, pl.ds((p % 2) * cols, cols)], train.at[p], train_sem.at[p])

    def trainx_copy(q):
        return pltpu.make_async_copy(
            train_ref.at[q, :, pl.ds(feat - XCOLS, XCOLS)], trainx.at[q], trainx_sem.at[q])

    for q in range(XPIECES):
        prex_copy(q).start()
    for p in range(PIECES):
        pre_copy(p).start()
    for p in range(PIECES):
        train_copy(p).start()
    for q in range(XPIECES):
        trainx_copy(q).start()

    barrier = pltpu.get_barrier_semaphore()

    def greet(target):
        pl.semaphore_signal(barrier, inc=1, device_id=target, device_id_type=MESH)

    greet(device(right, z, core))
    greet(device(left, z, core))
    greet(device(x, z, 1 - core))
    greet(device(x, side, core))
    greet(device(x, across, core))
    for j in range(1, NG):
        greet((lax.rem(g + j, NG), row))
    pl.semaphore_wait(barrier, 5 + NG - 1)

    def remote(ref, send_sem, recv_sem, target):
        return pltpu.make_async_remote_copy(
            src_ref=ref, dst_ref=ref, send_sem=send_sem, recv_sem=recv_sem,
            device_id=target, device_id_type=MESH)

    def xdev(d):
        return device(right if d == 0 else left, z, core)

    def xsrc(d):
        return left if d == 0 else right

    def part(d):
        return low if d == 0 else high

    partner = device(x, z, 1 - core)

    def to_side(k, k_there, p):
        return remote(held.at[held_z(k), p, core, x], zs.at[k_there, p], zr.at[k_there, p], device(x, side, core))

    def to_across(k, k_there, p):
        return remote(held.at[held_z(k), p, core, x], zs2.at[k_there, p], zr.at[k_there, p], device(x, across, core))

    def to_x(k, p, d):
        return remote(held.at[held_z(k), p, core, x], xs.at[d, k, p], xr.at[d, k, p], xdev(d))

    def from_x(k, p, d):
        return remote(held.at[held_z(k), p, core, xsrc(d)], xs.at[d, k, p], xr.at[d, k, p], xdev(d))

    def relay(k, p, d):
        return remote(held.at[held_z(k), p, core, xsrc(d), part(d)], hs.at[d, k, p], hr.at[d, k, p], xdev(d))

    def to_partner(k, p):
        return remote(held.at[held_z(k), p, core], ps.at[k, p], pr.at[k, p], partner)

    def wide_to_x(q, d):
        return remote(heldx.at[z, q, core, x], axs.at[d, q], axr.at[d, q], xdev(d))

    def wide_from_x(q, d):
        return remote(heldx.at[z, q, core, xsrc(d)], axs.at[d, q], axr.at[d, q], xdev(d))

    def wide_relay(q, d):
        return remote(heldx.at[z, q, core, xsrc(d), part(d)], ahs.at[d, q], ahr.at[d, q], xdev(d))

    def wide_to_side(k, k_there, q):
        return remote(heldx.at[held_z(k), q, core], bs.at[k_there, q], br.at[k_there, q], device(x, side, core))

    def wide_to_across(k, k_there, q):
        return remote(heldx.at[held_z(k), q, core], bs2.at[k_there, q], br.at[k_there, q], device(x, across, core))

    def wide_to_partner(k, q):
        return remote(heldx.at[held_z(k), q, core], aps.at[k, q], apr.at[k, q], partner)

    def to_y(k, t, b, dy):
        return pltpu.make_async_remote_copy(
            src_ref=stage_y.at[k, t], dst_ref=landed_y.at[b, y], send_sem=ys.at[k, t], recv_sem=yr.at[b, y],
            device_id=(zh * NY + dy, row), device_id_type=MESH)

    def from_y(b, sy):
        return pltpu.make_async_remote_copy(
            src_ref=stage_y.at[0, 0], dst_ref=landed_y.at[b, sy], send_sem=ys.at[0, 0], recv_sem=yr.at[b, sy],
            device_id=(zh * NY + sy, row), device_id_type=MESH)

    def to_z(b):
        return pltpu.make_async_remote_copy(
            src_ref=stage_z.at[b], dst_ref=landed_z.at[b], send_sem=ws.at[b], recv_sem=wr.at[b],
            device_id=((1 - zh) * NY + y, row), device_id_type=MESH)

    def to_owner(xx, owner):
        return pltpu.make_async_remote_copy(
            src_ref=stage_d.at[xx], dst_ref=landed_d.at[g], send_sem=ds.at[xx], recv_sem=dr.at[g],
            device_id=(owner, row), device_id_type=MESH)

    def from_member(src):
        return pltpu.make_async_remote_copy(
            src_ref=stage_d.at[0], dst_ref=landed_d.at[src], send_sem=ds.at[0], recv_sem=dr.at[src],
            device_id=(src, row), device_id_type=MESH)

    for q in range(XPIECES):
        prex_copy(q).wait()
        for d in range(2):
            wide_to_x(q, d).start()
    for p in range(PIECES):
        pre_copy(p).wait()
        to_side(0, 1, p).start()

        @pl.when(inner)
        def _():
            to_across(0, 2, p).start()

    def along_z(i):
        early = i - 2
        late = i - 4

        @pl.when(jnp.logical_and(inner, jnp.logical_and(early >= 0, early < PIECES)))
        def _():
            to_side(1, 1, early).wait_recv()
            to_across(1, 3, early).start()
            to_across(2, 2, early).wait_recv()
            to_side(2, 2, early).start()

        @pl.when(jnp.logical_and(inner, jnp.logical_and(late >= 0, late < PIECES)))
        def _():
            to_across(3, 3, late).wait_recv()
            to_side(3, 3, late).start()

    def wide(i):
        @pl.when(i == 1)
        def _():
            for q in range(XPIECES):
                for d in range(2):
                    wide_from_x(q, d).wait_recv()
                    wide_relay(q, d).start()

        @pl.when(i == 2)
        def _():
            for q in range(XPIECES):
                for d in range(2):
                    wide_relay(q, d).wait_recv()
                wide_to_side(0, 1, q).start()

                @pl.when(inner)
                def _():
                    wide_to_across(0, 2, q).start()

                wide_to_partner(0, q).start()

        @pl.when(i == 6)
        def _():
            for q in range(XPIECES):
                wide_to_side(1, 1, q).wait_recv()

                @pl.when(inner)
                def _():
                    wide_to_across(1, 3, q).start()
                    wide_to_across(2, 2, q).wait_recv()
                    wide_to_side(2, 2, q).start()
                    wide_to_partner(2, q).start()

                wide_to_partner(1, q).start()

        @pl.when(jnp.logical_and(i == 10, inner))
        def _():
            for q in range(XPIECES):
                wide_to_across(3, 3, q).wait_recv()
                wide_to_side(3, 3, q).start()
                wide_to_partner(3, q).start()

        @pl.when(jnp.logical_and(i == 12, end))
        def _():
            for q in range(XPIECES):
                wide_to_side(2, 2, q).wait_recv()
                wide_to_partner(2, q).start()

        @pl.when(jnp.logical_and(i == 16, end))
        def _():
            for q in range(XPIECES):
                wide_to_side(3, 3, q).wait_recv()
                wide_to_partner(3, q).start()

    def sums_of(xx):
        return [acc[pl.ds((c * NX + xx) * rows, rows), :] for c in range(2)]

    def send_sums(k):
        zz = held_z(k)
        b = lax.rem(zz, 2)

        @pl.when(k < NZ - 1)
        def _():
            for t in range(2):
                dy = 2 * t + zz // 2

                @pl.when(dy == y)
                def _():
                    for h in range(2):
                        for c, value in enumerate(sums_of(2 * h + t)):
                            mine[b, h, pl.ds(c * rows, rows), :] = value

                @pl.when(dy != y)
                def _():
                    for h in range(2):
                        for c, value in enumerate(sums_of(2 * h + t)):
                            stage_y[k, t, h, pl.ds(c * rows, rows), :] = value.astype(jnp.bfloat16)
                    to_y(k, t, b, dy).start()

        @pl.when(k == NZ - 1)
        def _():
            for xx in range(NX):
                owner = 2 * xx + zz // 2

                @pl.when(owner == g)
                def _():
                    for c, value in enumerate(sums_of(xx)):
                        mine[b, zh, pl.ds(c * rows, rows), :] = value

                @pl.when(owner != g)
                def _():
                    for c, value in enumerate(sums_of(xx)):
                        stage_d[xx, pl.ds(c * rows, rows), :] = value.astype(jnp.bfloat16)
                    to_owner(xx, owner).start()

    def reduce_y(i):
        k = (i - 9) // PIECES

        @pl.when(jnp.logical_and(i >= 9, jnp.logical_and(lax.rem(i - 9 + PIECES, PIECES) == 0, k < NZ - 1)))
        def _():
            zz = held_z(k)
            b = lax.rem(zz, 2)

            @pl.when(zz // 2 == lax.rem(y, 2))
            def _():
                for j in range(1, NY):
                    from_y(b, lax.rem(y + j, NY)).wait_recv()

                def total(h):
                    value = mine[b, h]
                    for j in range(1, NY):
                        value = value + landed_y[b, lax.rem(y + j, NY), h].astype(jnp.float32)
                    return value

                stage_z[b] = total(1 - zh).astype(jnp.bfloat16)
                to_z(b).start()
                mine[b, zh] = total(zh)

    def step(i, carry):
        along_z(i)
        wide(i)

        @pl.when(i < STEPS)
        def _():
            k, p = i // PIECES, lax.rem(i, PIECES)

            @pl.when(jnp.logical_and(end, k > 0))
            def _():
                to_side(k, k, p).wait_recv()

            to_x(k, p, 0).start()
            to_x(k, p, 1).start()

        @pl.when(jnp.logical_and(i >= 1, i < STEPS + 1))
        def _():
            s = i - 1
            k, p = s // PIECES, lax.rem(s, PIECES)
            from_x(k, p, 0).wait_recv()
            relay(k, p, 0).start()
            from_x(k, p, 1).wait_recv()
            relay(k, p, 1).start()

        @pl.when(jnp.logical_and(i >= 2, i < STEPS + 2))
        def _():
            s = i - 2
            k, p = s // PIECES, lax.rem(s, PIECES)
            relay(k, p, 0).wait_recv()
            relay(k, p, 1).wait_recv()
            to_partner(k, p).start()

        @pl.when(i >= 3)
        def _():
            s = i - 3
            k, p = s // PIECES, lax.rem(s, PIECES)

            def product(lhs, rhs):
                return lax.dot_general(lhs.reshape(2 * NX * rows, lhs.shape[-1]), rhs, (((1,), (1,)), ((), ())),
                                       preferred_element_type=jnp.float32)

            @pl.when(p == 0)
            def _():
                for q in range(XPIECES):
                    @pl.when(k == 0)
                    def _():
                        trainx_copy(q).wait()

            @pl.when(k == 0)
            def _():
                pltpu.make_async_copy(train.at[p], train.at[p], train_sem.at[p]).wait()

            to_partner(k, p).wait_recv()
            term = product(held[held_z(k), p], train[p])

            @pl.when(p == 0)
            def _():
                acc[...] = term

            @pl.when(p > 0)
            def _():
                acc[...] += term

            @pl.when(p == PIECES - 1)
            def _():
                for q in range(XPIECES):
                    wide_to_partner(k, q).wait_recv()
                    acc[...] += product(heldx[held_z(k), q], trainx[q])
                send_sums(k)

        reduce_y(i)
        return carry

    lax.fori_loop(0, STEPS + 3, step, 0)

    late_owner = lax.rem(y, 2) != upper
    last_b = lax.rem(held_z(NZ - 1), 2)
    block = 2 * rows
    for b in range(2):
        direct = jnp.logical_and(late_owner, last_b == b)
        place = pl.ds(b * block, block)

        @pl.when(jnp.logical_not(direct))
        def _():
            to_z(b).wait_recv()
            out_ref[place, :] = mine[b, zh] + landed_z[b].astype(jnp.float32)

        @pl.when(direct)
        def _():
            out_ref[place, :] = mine[b, zh]
            for j in range(1, NG):
                src = lax.rem(g + j, NG)
                from_member(src).wait_recv()
                out_ref[place, :] += landed_d[src].astype(jnp.float32)

    def drain(s, carry):
        k, p = s // PIECES, lax.rem(s, PIECES)
        for d in range(2):
            to_x(k, p, d).wait_send()
            relay(k, p, d).wait_send()
        to_partner(k, p).wait_send()

        @pl.when(k == 0)
        def _():
            to_side(0, 1, p).wait_send()

        @pl.when(inner)
        def _():
            @pl.when(k == 0)
            def _():
                to_across(0, 2, p).wait_send()

            @pl.when(k == 1)
            def _():
                to_across(1, 3, p).wait_send()

            @pl.when(k >= 2)
            def _():
                to_side(k, k, p).wait_send()

        return carry

    lax.fori_loop(0, STEPS, drain, 0)
    for q in range(XPIECES):
        for d in range(2):
            wide_to_x(q, d).wait_send()
            wide_relay(q, d).wait_send()
        wide_to_side(0, 1, q).wait_send()
        for k in range(NZ):
            wide_to_partner(k, q).wait_send()

        @pl.when(inner)
        def _():
            wide_to_across(0, 2, q).wait_send()
            wide_to_across(1, 3, q).wait_send()
            wide_to_side(2, 2, q).wait_send()
            wide_to_side(3, 3, q).wait_send()

    for k in range(NZ - 1):
        zz = held_z(k)
        for t in range(2):
            @pl.when(2 * t + zz // 2 != y)
            def _():
                to_y(k, t, 0, 0).wait_send()

    for b in range(2):
        @pl.when(jnp.logical_not(jnp.logical_and(late_owner, last_b == b)))
        def _():
            to_z(b).wait_send()

    for xx in range(NX):
        @pl.when(2 * xx + held_z(NZ - 1) // 2 != g)
        def _():
            to_owner(xx, 0).wait_send()


def scores_of(pre, train_grads):
    layers, rows, feat = pre.shape
    train_rows = train_grads.shape[1]
    cols = (feat - XCOLS) * layers // PIECES
    block = NX * NZ * 2 * rows // NG
    dma = pltpu.SemaphoreType.DMA
    bf16, f32 = jnp.bfloat16, jnp.float32
    return pl.pallas_call(
        kernel,
        out_shape=jax.ShapeDtypeStruct((block, train_rows), f32),
        in_specs=[pl.BlockSpec(memory_space=pl.ANY)] * 2,
        out_specs=pl.BlockSpec(memory_space=pltpu.VMEM),
        scratch_shapes=[
            pltpu.VMEM((NZ, PIECES, 2, NX, rows, cols), bf16),
            pltpu.VMEM((NZ, XPIECES, 2, NX, rows, XCOLS), bf16),
            pltpu.VMEM((PIECES, train_rows, cols), bf16),
            pltpu.VMEM((XPIECES, train_rows, XCOLS), bf16),
            pltpu.VMEM((2 * NX * rows, train_rows), f32),
            pltpu.VMEM((2, 2, 2 * rows, train_rows), f32),
            pltpu.VMEM((NZ - 1, 2, 2, 2 * rows, train_rows), bf16),
            pltpu.VMEM((2, NY, 2, 2 * rows, train_rows), bf16),
            pltpu.VMEM((2, 2 * rows, train_rows), bf16),
            pltpu.VMEM((2, 2 * rows, train_rows), bf16),
            pltpu.VMEM((NX, 2 * rows, train_rows), bf16),
            pltpu.VMEM((NG, 2 * rows, train_rows), bf16),
            dma((PIECES,)), dma((XPIECES,)), dma((PIECES,)), dma((XPIECES,)),
            dma((NZ, PIECES)), dma((NZ, PIECES)), dma((NZ, PIECES)),
            dma((2, NZ, PIECES)), dma((2, NZ, PIECES)), dma((2, NZ, PIECES)), dma((2, NZ, PIECES)),
            dma((NZ, PIECES)), dma((NZ, PIECES)),
            dma((NZ, XPIECES)), dma((NZ, XPIECES)), dma((NZ, XPIECES)),
            dma((2, XPIECES)), dma((2, XPIECES)), dma((2, XPIECES)), dma((2, XPIECES)),
            dma((NZ, XPIECES)), dma((NZ, XPIECES)),
            dma((NZ - 1, 2)), dma((2, NY)), dma((2,)), dma((2,)), dma((NX,)), dma((NG,)),
        ],
        compiler_params=pltpu.CompilerParams(
            collective_id=0, has_side_effects=True, vmem_limit_bytes=60 * 1024 * 1024),
    )(pre, train_grads)


def on_device(query_grads, train_grads, left_inverse, right_inverse):
    layers, rows, feat = query_grads.shape
    proj = left_inverse.shape[1]
    square = query_grads.astype(jnp.float32).reshape(layers, rows, proj, proj)
    rotated = jnp.einsum(
        "lab,lqbc,lcd->lqad", left_inverse, square, right_inverse, precision=lax.Precision.HIGHEST
    )
    rotated = rotated.reshape(layers, rows, feat).astype(jnp.bfloat16)
    return scores_of(rotated, train_grads)


def solution(mesh):
    placed = (
        P("layer", "row", None),
        P("layer", "row", None),
        P("layer", None, None),
        P("layer", None, None),
    )
    return jax.shard_map(
        on_device, mesh=mesh, in_specs=placed, out_specs=P("layer", "row"), check_vma=False
    )
```

time: 104 us -> 102 us (0.981)
  the two profiles are of different devices: /device:TPU:24 before, /device:TPU:59 now
where the time goes in v2:
time: 102 us; the launch traced here: 101 us
  Pallas kernels  93.2 us (91%)
  local copies, waits for them, and re-layouts  5.37 us (5%)
  matrix products  2.86 us (3%)
    pallas_call x1, Pallas kernels, scores_of(): pl.pallas_call(kernel, out_shape=jax.ShapeDtypeStruct((block, train_rows)...  93.2 us
    dot_general x2, matrix products, on_device(): jnp.einsum('lab,lqbc,lcd->lqad', left_inverse, square, right_inverse, pre...  2.86 us
    reshape x1, local copies, waits for them, and re-layouts, on_device(): square = query_grads.astype(jnp.float32).reshape(layers, rows, proj, proj)  2.09 us

profile of v2, /device:TPU:59, one launch (start us, length us, event | category | flops | bytes accessed | tf_op | source)
XLA Modules:
  0.0 101.5 jit_solution(16690455494865341787)
XLA Ops:
  0.0 0.0 copy-start
  0.0 0.0 copy-start.1
  0.0 2.1 %reshape.5 = bf16[2,32,64,64]{3,2,1,0:T(8,128)(2,1)S(1)} reshape(bf16[2,32,4096]{2,1,0:T(8,128)(2,1)} %param.4) | data formatting | bytes 1048576 | tf_op jit(solution)/shard_map/reshape | solution.py:505
  2.1 0.0 copy-done
  2.1 1.0 fusion.1
  3.1 0.0 copy-done.1
  3.1 1.9 %convolution_convert_fusion = bf16[2,32,64,64]{3,2,1,0:T(8,128)(2,1)S(1)} fusion(f32[2,32,64,64]{2,3,1,0:T(8,128)S(1)} %fusion.1, f32[2,64,64]{2,1,0:T(8,128)S(1)} %copy-done.1), kind=kOutput, calls=%fused_computation | convolution fusion | flops 201588736 | bytes 1605632 | tf_op jit(solution)/shard_map/lab,lqbc,lcd->lqad/dot_general | solution.py:506
  5.0 1.6 %convert_element_type.7.pre_ref = bf16[2,32,4096]{2,1,0:T(8,128)(2,1)} reshape(bf16[2,32,64,64]{3,2,1,0:T(8,128)(2,1)S(1)} %convolution_convert_fusion) | data formatting | bytes 1048576 | tf_op jit(solution)/shard_map/convert_element_type | solution.py:509
  6.6 93.2 %shard_map.46 = f32[128,512]{1,0:T(8,128)} custom-call(bf16[2,32,4096]{2,1,0:T(8,128)(2,1)} %convert_element_type.7.pre_ref, bf16[2,512,4096]{2,1,0:T(8,128)(2,1)} %train_ref.1), custom_call_target="tpu_custom_call" | custom-call | tf_op jit(solution)/shard_map/pallas_call | solution.py:470
  99.8 1.7 %copy.8 = f32[128,512]{1,0:T(8,128)} copy(f32[128,512]{1,0:T(8,128)} %shard_map.46) | data formatting | bytes 524288
Async XLA Ops:
  0.0 2.1 %copy-start = (f32[2,64,64]{2,1,0:T(8,128)S(1)}, f32[2,64,64]{2,1,0:T(8,128)}, u32[]{:S(2)}) copy-start(f32[2,64,64]{2,1,0:T(8,128)} %param.6) | copy-start | bytes 98308
  0.0 3.1 %copy-start.1 = (f32[2,64,64]{2,1,0:T(8,128)S(1)}, f32[2,64,64]{2,1,0:T(8,128)}, u32[]{:S(2)}) copy-start(f32[2,64,64]{2,1,0:T(8,128)} %param.7) | copy-start | bytes 98308

commit v3 on v2

--- a/solution.py
+++ b/solution.py
@@ -11,10 +11,77 @@
 STEPS = NZ * PIECES
 XPIECES = 2
 XCOLS = 768
-
-
-def kernel(pre_ref, train_ref, out_ref, held, heldx, train, trainx, acc, mine, stage_y, landed_y, stage_z, landed_z,
-           stage_d, landed_d, pre_sem, prex_sem, train_sem, trainx_sem, zs, zs2, zr, xs, xr, hs, hr, ps, pr,
+AT_B, AT_C, AT_D, AT_SUM = 2, 4, 5, 11
+
+
+def split(value):
+    high = value.astype(jnp.bfloat16)
+    return high, (value - high.astype(jnp.float32)).astype(jnp.bfloat16)
+
+
+def matmul(a, b):
+    return jnp.dot(a, b, preferred_element_type=jnp.float32)
+
+
+def precondition(query, left, right, turned, result, store):
+    rows, feat = query.shape
+    proj = left.shape[0]
+    pairs = proj // 2
+    lanes = 2 * proj
+    bf16, f32 = jnp.bfloat16, jnp.float32
+
+    def iota(shape, axis):
+        return lax.broadcasted_iota(jnp.int32, shape, axis)
+
+    def ones_where(mask):
+        return jnp.where(mask, 1.0, 0.0).astype(bf16)
+
+    twice = ones_where(iota((proj, lanes), 1) % proj == iota((proj, lanes), 0))
+    same_half = iota((lanes, lanes), 0) // proj == iota((lanes, lanes), 1) // proj
+
+    def block_diagonal(part):
+        wide = matmul(part, twice)
+        return jnp.where(same_half, jnp.concatenate([wide, wide], axis=0), 0.0).astype(bf16)
+
+    right_high, right_low = split(right[...])
+    factor = jnp.concatenate([block_diagonal(right_high), block_diagonal(right_low)], axis=1)
+    stacked = jnp.concatenate([query[:, lanes * j:lanes * (j + 1)] for j in range(pairs)], axis=0)
+    both = matmul(stacked, factor)
+    turned[...] = both[:, :lanes] + both[:, lanes:]
+
+    pick = ones_where(iota((proj, proj), 1) == 2 * (iota((proj, proj), 0) % pairs) + iota((proj, proj), 0) // pairs)
+    b, place = iota((proj, proj), 0), iota((proj, proj), 1)
+    other, j = place // pairs, place % pairs
+    even = ones_where(b == 2 * j + other)
+    odd = ones_where(b == 2 * j + 1 - other)
+    upper_rows = iota((proj, proj), 0) < pairs
+
+    def arranged(part):
+        picked = matmul(pick, part).astype(bf16)
+        return jnp.where(upper_rows, matmul(picked, even), matmul(picked, odd)).astype(bf16)
+
+    left_high, left_low = split(left[...])
+    high, low = arranged(left_high), arranged(left_low)
+    weights = jnp.concatenate([
+        jnp.concatenate([high, high], axis=1),
+        jnp.concatenate([low, jnp.zeros_like(low)], axis=1)], axis=0)
+    group = 8
+    first_half = iota((pairs, lanes * group), 1) % lanes < proj
+    for start in range(0, rows, group):
+        own = [turned[pl.ds(q, pairs, stride=rows), :] for q in range(start, start + group)]
+        own_high, own_low = split(jnp.concatenate(own, axis=1))
+        rolled_high, rolled_low = split(jnp.concatenate([pltpu.roll(v, proj, 1) for v in own], axis=1))
+        value = matmul(weights, jnp.concatenate([own_high, rolled_high, own_low, rolled_low], axis=0))
+        value = value[:proj] + value[proj:]
+        value = jnp.where(first_half, value[:pairs], value[pairs:])
+        for q in range(group):
+            result[pl.ds((start + q) * pairs, pairs), :] = value[:, lanes * q:lanes * (q + 1)]
+    for i in range(pairs):
+        store(i, result[pl.ds(i, rows, stride=pairs), :].astype(bf16))
+
+
+def kernel(query_ref, left_ref, right_ref, train_ref, out_ref, query, left_v, right_v, turned, result, held, heldx, train, trainx, acc, mine, stage_y, landed_y, stage_z, landed_z,
+           stage_d, landed_d, in_sem, train_sem, trainx_sem, zs, zs2, zr, xs, xr, hs, hr, ps, pr,
            bs, bs2, br, axs, axr, ahs, ahr, aps, apr, ys, yr, ws, wr, ds, dr):
     g = lax.axis_index("layer")
     row = lax.axis_index("row")
@@ -30,8 +97,7 @@
     right, left = lax.rem(x + 1, NX), lax.rem(x + NX - 1, NX)
     side = z + 1 - 2 * lax.rem(z, 2)
     across = 3 - z
-    rows = pre_ref.shape[1]
-    feat = pre_ref.shape[2]
+    layers, rows, feat = query_ref.shape
     cols = held.shape[-1]
     low, high = pl.ds(0, rows // 2), pl.ds(rows // 2, rows // 2)
 
@@ -42,13 +108,9 @@
         c = jnp.where(k == 0, zl, jnp.where(k == 1, 1 - zl, k))
         return jnp.where(upper == 1, 3 - c, c)
 
-    def pre_copy(p):
-        return pltpu.make_async_copy(
-            pre_ref.at[p // 2, :, pl.ds((p % 2) * cols, cols)], held.at[z, p, core, x], pre_sem.at[p])
-
-    def prex_copy(q):
-        return pltpu.make_async_copy(
-            pre_ref.at[q, :, pl.ds(feat - XCOLS, XCOLS)], heldx.at[z, q, core, x], prex_sem.at[q])
+    def in_copies():
+        return [pltpu.make_async_copy(src, dst, in_sem.at[n]) for n, (src, dst) in enumerate(
+            ((query_ref, query), (left_ref, left_v), (right_ref, right_v)))]
 
     def train_copy(p):
         return pltpu.make_async_copy(
@@ -58,10 +120,8 @@
         return pltpu.make_async_copy(
             train_ref.at[q, :, pl.ds(feat - XCOLS, XCOLS)], trainx.at[q], trainx_sem.at[q])
 
-    for q in range(XPIECES):
-        prex_copy(q).start()
-    for p in range(PIECES):
-        pre_copy(p).start()
+    for copy in in_copies():
+        copy.start()
     for p in range(PIECES):
         train_copy(p).start()
     for q in range(XPIECES):
@@ -79,6 +139,20 @@
     greet(device(x, across, core))
     for j in range(1, NG):
         greet((lax.rem(g + j, NG), row))
+
+    for copy in in_copies():
+        copy.wait()
+    tiles = cols // 128
+    for layer in range(layers):
+        def store(i, value):
+            n, at = i // tiles, (i % tiles) * 128
+            if n < PIECES // layers:
+                held[z, layer * (PIECES // layers) + n, core, x, :, at:at + 128] = value
+            else:
+                heldx[z, layer, core, x, :, at:at + 128] = value
+
+        precondition(query.at[layer], left_v.at[layer], right_v.at[layer], turned, result, store)
+
     pl.semaphore_wait(barrier, 5 + NG - 1)
 
     def remote(ref, send_sem, recv_sem, target):
@@ -159,11 +233,9 @@
             device_id=(src, row), device_id_type=MESH)
 
     for q in range(XPIECES):
-        prex_copy(q).wait()
         for d in range(2):
             wide_to_x(q, d).start()
     for p in range(PIECES):
-        pre_copy(p).wait()
         to_side(0, 1, p).start()
 
         @pl.when(inner)
@@ -171,8 +243,8 @@
             to_across(0, 2, p).start()
 
     def along_z(i):
-        early = i - 2
-        late = i - 4
+        early = i - 4
+        late = i - 9
 
         @pl.when(jnp.logical_and(inner, jnp.logical_and(early >= 0, early < PIECES)))
         def _():
@@ -194,7 +266,7 @@
                     wide_from_x(q, d).wait_recv()
                     wide_relay(q, d).start()
 
-        @pl.when(i == 2)
+        @pl.when(i == 3)
         def _():
             for q in range(XPIECES):
                 for d in range(2):
@@ -207,34 +279,40 @@
 
                 wide_to_partner(0, q).start()
 
-        @pl.when(i == 6)
-        def _():
-            for q in range(XPIECES):
-                wide_to_side(1, 1, q).wait_recv()
-
+        @pl.when(i == 8)
+        def _():
+            for q in range(XPIECES):
                 @pl.when(inner)
                 def _():
-                    wide_to_across(1, 3, q).start()
                     wide_to_across(2, 2, q).wait_recv()
                     wide_to_side(2, 2, q).start()
                     wide_to_partner(2, q).start()
 
+        @pl.when(i == 9)
+        def _():
+            for q in range(XPIECES):
+                wide_to_side(1, 1, q).wait_recv()
+
+                @pl.when(inner)
+                def _():
+                    wide_to_across(1, 3, q).start()
+
                 wide_to_partner(1, q).start()
 
-        @pl.when(jnp.logical_and(i == 10, inner))
+        @pl.when(jnp.logical_and(i == 14, inner))
         def _():
             for q in range(XPIECES):
                 wide_to_across(3, 3, q).wait_recv()
                 wide_to_side(3, 3, q).start()
                 wide_to_partner(3, q).start()
 
-        @pl.when(jnp.logical_and(i == 12, end))
+        @pl.when(jnp.logical_and(i == 15, end))
         def _():
             for q in range(XPIECES):
                 wide_to_side(2, 2, q).wait_recv()
                 wide_to_partner(2, q).start()
 
-        @pl.when(jnp.logical_and(i == 16, end))
+        @pl.when(jnp.logical_and(i == 17, end))
         def _():
             for q in range(XPIECES):
                 wide_to_side(3, 3, q).wait_recv()
@@ -282,9 +360,9 @@
                     to_owner(xx, owner).start()
 
     def reduce_y(i):
-        k = (i - 9) // PIECES
-
-        @pl.when(jnp.logical_and(i >= 9, jnp.logical_and(lax.rem(i - 9 + PIECES, PIECES) == 0, k < NZ - 1)))
+        k = (i - AT_SUM) // PIECES
+
+        @pl.when(jnp.logical_and(i >= AT_SUM, jnp.logical_and(lax.rem(i - AT_SUM + NZ * PIECES, PIECES) == 0, k < NZ - 1)))
         def _():
             zz = held_z(k)
             b = lax.rem(zz, 2)
@@ -319,26 +397,26 @@
             to_x(k, p, 0).start()
             to_x(k, p, 1).start()
 
-        @pl.when(jnp.logical_and(i >= 1, i < STEPS + 1))
-        def _():
-            s = i - 1
+        @pl.when(jnp.logical_and(i >= AT_B, i < STEPS + AT_B))
+        def _():
+            s = i - AT_B
             k, p = s // PIECES, lax.rem(s, PIECES)
             from_x(k, p, 0).wait_recv()
             relay(k, p, 0).start()
             from_x(k, p, 1).wait_recv()
             relay(k, p, 1).start()
 
-        @pl.when(jnp.logical_and(i >= 2, i < STEPS + 2))
-        def _():
-            s = i - 2
+        @pl.when(jnp.logical_and(i >= AT_C, i < STEPS + AT_C))
+        def _():
+            s = i - AT_C
             k, p = s // PIECES, lax.rem(s, PIECES)
             relay(k, p, 0).wait_recv()
             relay(k, p, 1).wait_recv()
             to_partner(k, p).start()
 
-        @pl.when(i >= 3)
-        def _():
-            s = i - 3
+        @pl.when(i >= AT_D)
+        def _():
+            s = i - AT_D
             k, p = s // PIECES, lax.rem(s, PIECES)
 
             def product(lhs, rhs):
@@ -377,7 +455,7 @@
         reduce_y(i)
         return carry
 
-    lax.fori_loop(0, STEPS + 3, step, 0)
+    lax.fori_loop(0, STEPS + AT_D, step, 0)
 
     late_owner = lax.rem(y, 2) != upper
     last_b = lax.rem(held_z(NZ - 1), 2)
@@ -460,8 +538,9 @@
             to_owner(xx, 0).wait_send()
 
 
-def scores_of(pre, train_grads):
-    layers, rows, feat = pre.shape
+def on_device(query_grads, train_grads, left_inverse, right_inverse):
+    layers, rows, feat = query_grads.shape
+    proj = left_inverse.shape[1]
     train_rows = train_grads.shape[1]
     cols = (feat - XCOLS) * layers // PIECES
     block = NX * NZ * 2 * rows // NG
@@ -470,9 +549,14 @@
     return pl.pallas_call(
         kernel,
         out_shape=jax.ShapeDtypeStruct((block, train_rows), f32),
-        in_specs=[pl.BlockSpec(memory_space=pl.ANY)] * 2,
+        in_specs=[pl.BlockSpec(memory_space=pl.ANY)] * 4,
         out_specs=pl.BlockSpec(memory_space=pltpu.VMEM),
         scratch_shapes=[
+            pltpu.VMEM((layers, rows, feat), bf16),
+            pltpu.VMEM((layers, proj, proj), f32),
+            pltpu.VMEM((layers, proj, proj), f32),
+            pltpu.VMEM((rows * proj // 2, 2 * proj), f32),
+            pltpu.VMEM((rows * proj // 2, 2 * proj), f32),
             pltpu.VMEM((NZ, PIECES, 2, NX, rows, cols), bf16),
             pltpu.VMEM((NZ, XPIECES, 2, NX, rows, XCOLS), bf16),
             pltpu.VMEM((PIECES, train_rows, cols), bf16),
@@ -485,7 +569,7 @@
             pltpu.VMEM((2, 2 * rows, train_rows), bf16),
             pltpu.VMEM((NX, 2 * rows, train_rows), bf16),
             pltpu.VMEM((NG, 2 * rows, train_rows), bf16),
-            dma((PIECES,)), dma((XPIECES,)), dma((PIECES,)), dma((XPIECES,)),
+            dma((3,)), dma((PIECES,)), dma((XPIECES,)),
             dma((NZ, PIECES)), dma((NZ, PIECES)), dma((NZ, PIECES)),
             dma((2, NZ, PIECES)), dma((2, NZ, PIECES)), dma((2, NZ, PIECES)), dma((2, NZ, PIECES)),
             dma((NZ, PIECES)), dma((NZ, PIECES)),
@@ -496,18 +580,7 @@
         ],
         compiler_params=pltpu.CompilerParams(
             collective_id=0, has_side_effects=True, vmem_limit_bytes=60 * 1024 * 1024),
-    )(pre, train_grads)
-
-
-def on_device(query_grads, train_grads, left_inverse, right_inverse):
-    layers, rows, feat = query_grads.shape
-    proj = left_inverse.shape[1]
-    square = query_grads.astype(jnp.float32).reshape(layers, rows, proj, proj)
-    rotated = jnp.einsum(
-        "lab,lqbc,lcd->lqad", left_inverse, square, right_inverse, precision=lax.Precision.HIGHEST
-    )
-    rotated = rotated.reshape(layers, rows, feat).astype(jnp.bfloat16)
-    return scores_of(rotated, train_grads)
+    )(query_grads, left_inverse, right_inverse, train_grads)
 
 
 def solution(mesh):

time: 102 us -> 91.4 us (0.90)
  the two profiles are of different devices: /device:TPU:59 before, /device:TPU:24 now
where the time goes in v3:
time: 91.4 us; the launch traced here: 91.1 us
  Pallas kernels  89.4 us (98%)
  local copies, waits for them, and re-layouts  1.67 us (2%)
    pallas_call x1, Pallas kernels, on_device(): pl.pallas_call(kernel, out_shape=jax.ShapeDtypeStruct((block, train_rows)...  89.4 us

profile of v3, /device:TPU:24, one launch (start us, length us, event | category | flops | bytes accessed | tf_op | source)
XLA Modules:
  0.0 91.1 jit_solution(5369469141153207931)
XLA Ops:
  0.0 89.4 %shard_map.46 = f32[128,512]{1,0:T(8,128)} custom-call(bf16[2,32,4096]{2,1,0:T(8,128)(2,1)} %query_ref.1, f32[2,64,64]{2,1,0:T(8,128)} %left_ref.1, f32[2,64,64]{2,1,0:T(8,128)} %right_ref.1, bf16[2,512,4096]{2,1,0:T(8,128)(2,1)} %train_ref.1), custom_call_target="tpu_custom_call" | custom-call | tf_op jit(solution)/shard_map/pallas_call | solution.py:549
  89.4 1.7 %copy.6 = f32[128,512]{1,0:T(8,128)} copy(f32[128,512]{1,0:T(8,128)} %shard_map.46) | data formatting | bytes 524288

commit v4 on v3

--- a/solution.py
+++ b/solution.py
@@ -11,7 +11,8 @@
 STEPS = NZ * PIECES
 XPIECES = 2
 XCOLS = 768
-AT_B, AT_C, AT_D, AT_SUM = 2, 4, 5, 11
+HALVES = 2
+AT_B, AT_C, AT_D, AT_SUM = 2, 4, 5, 8
 
 
 def split(value):
@@ -99,7 +100,9 @@
     across = 3 - z
     layers, rows, feat = query_ref.shape
     cols = held.shape[-1]
-    low, high = pl.ds(0, rows // 2), pl.ds(rows // 2, rows // 2)
+    few = rows // HALVES
+    low, high = pl.ds(0, cols // 2), pl.ds(cols // 2, cols // 2)
+    wide_low, wide_high = pl.ds(0, few), pl.ds(few, few)
 
     def device(xx, zz, cc):
         return (g, (xx * NZ + zz) * 2 + cc)
@@ -114,7 +117,7 @@
 
     def train_copy(p):
         return pltpu.make_async_copy(
-            train_ref.at[p // 2, :, pl.ds((p % 2) * cols, cols)], train.at[p], train_sem.at[p])
+            train_ref.at[p, :, pl.ds(0, cols)], train.at[p], train_sem.at[p])
 
     def trainx_copy(q):
         return pltpu.make_async_copy(
@@ -122,7 +125,7 @@
 
     for copy in in_copies():
         copy.start()
-    for p in range(PIECES):
+    for p in range(layers):
         train_copy(p).start()
     for q in range(XPIECES):
         trainx_copy(q).start()
@@ -145,10 +148,11 @@
     tiles = cols // 128
     for layer in range(layers):
         def store(i, value):
-            n, at = i // tiles, (i % tiles) * 128
-            if n < PIECES // layers:
-                held[z, layer * (PIECES // layers) + n, core, x, :, at:at + 128] = value
+            if i < tiles:
+                for h in range(HALVES):
+                    held[z, h * layers + layer, core, x, :, 128 * i:128 * (i + 1)] = value[h * few:(h + 1) * few]
             else:
+                at = 128 * (i - tiles)
                 heldx[z, layer, core, x, :, at:at + 128] = value
 
         precondition(query.at[layer], left_v.at[layer], right_v.at[layer], turned, result, store)
@@ -169,6 +173,9 @@
     def part(d):
         return low if d == 0 else high
 
+    def wide_part(d):
+        return wide_low if d == 0 else wide_high
+
     partner = device(x, z, 1 - core)
 
     def to_side(k, k_there, p):
@@ -184,7 +191,7 @@
         return remote(held.at[held_z(k), p, core, xsrc(d)], xs.at[d, k, p], xr.at[d, k, p], xdev(d))
 
     def relay(k, p, d):
-        return remote(held.at[held_z(k), p, core, xsrc(d), part(d)], hs.at[d, k, p], hr.at[d, k, p], xdev(d))
+        return remote(held.at[held_z(k), p, core, xsrc(d), :, part(d)], hs.at[d, k, p], hr.at[d, k, p], xdev(d))
 
     def to_partner(k, p):
         return remote(held.at[held_z(k), p, core], ps.at[k, p], pr.at[k, p], partner)
@@ -196,7 +203,7 @@
         return remote(heldx.at[z, q, core, xsrc(d)], axs.at[d, q], axr.at[d, q], xdev(d))
 
     def wide_relay(q, d):
-        return remote(heldx.at[z, q, core, xsrc(d), part(d)], ahs.at[d, q], ahr.at[d, q], xdev(d))
+        return remote(heldx.at[z, q, core, xsrc(d), wide_part(d)], ahs.at[d, q], ahr.at[d, q], xdev(d))
 
     def wide_to_side(k, k_there, q):
         return remote(heldx.at[held_z(k), q, core], bs.at[k_there, q], br.at[k_there, q], device(x, side, core))
@@ -207,29 +214,29 @@
     def wide_to_partner(k, q):
         return remote(heldx.at[held_z(k), q, core], aps.at[k, q], apr.at[k, q], partner)
 
-    def to_y(k, t, b, dy):
+    def to_y(k, h, t, b, dy):
         return pltpu.make_async_remote_copy(
-            src_ref=stage_y.at[k, t], dst_ref=landed_y.at[b, y], send_sem=ys.at[k, t], recv_sem=yr.at[b, y],
-            device_id=(zh * NY + dy, row), device_id_type=MESH)
-
-    def from_y(b, sy):
+            src_ref=stage_y.at[k, h, t], dst_ref=landed_y.at[b, h, y], send_sem=ys.at[k, h, t],
+            recv_sem=yr.at[b, h, y], device_id=(zh * NY + dy, row), device_id_type=MESH)
+
+    def from_y(b, h, sy):
         return pltpu.make_async_remote_copy(
-            src_ref=stage_y.at[0, 0], dst_ref=landed_y.at[b, sy], send_sem=ys.at[0, 0], recv_sem=yr.at[b, sy],
-            device_id=(zh * NY + sy, row), device_id_type=MESH)
-
-    def to_z(b):
+            src_ref=stage_y.at[0, 0, 0], dst_ref=landed_y.at[b, h, sy], send_sem=ys.at[0, 0, 0],
+            recv_sem=yr.at[b, h, sy], device_id=(zh * NY + sy, row), device_id_type=MESH)
+
+    def to_z(b, h):
         return pltpu.make_async_remote_copy(
-            src_ref=stage_z.at[b], dst_ref=landed_z.at[b], send_sem=ws.at[b], recv_sem=wr.at[b],
+            src_ref=stage_z.at[b, h], dst_ref=landed_z.at[b, h], send_sem=ws.at[b, h], recv_sem=wr.at[b, h],
             device_id=((1 - zh) * NY + y, row), device_id_type=MESH)
 
-    def to_owner(xx, owner):
+    def to_owner(h, xx, owner):
         return pltpu.make_async_remote_copy(
-            src_ref=stage_d.at[xx], dst_ref=landed_d.at[g], send_sem=ds.at[xx], recv_sem=dr.at[g],
+            src_ref=stage_d.at[h, xx], dst_ref=landed_d.at[h, g], send_sem=ds.at[h, xx], recv_sem=dr.at[h, g],
             device_id=(owner, row), device_id_type=MESH)
 
-    def from_member(src):
+    def from_member(h, src):
         return pltpu.make_async_remote_copy(
-            src_ref=stage_d.at[0], dst_ref=landed_d.at[src], send_sem=ds.at[0], recv_sem=dr.at[src],
+            src_ref=stage_d.at[0, 0], dst_ref=landed_d.at[h, src], send_sem=ds.at[0, 0], recv_sem=dr.at[h, src],
             device_id=(src, row), device_id_type=MESH)
 
     for q in range(XPIECES):
@@ -243,8 +250,8 @@
             to_across(0, 2, p).start()
 
     def along_z(i):
-        early = i - 4
-        late = i - 9
+        early = i - 3
+        late = i - 8
 
         @pl.when(jnp.logical_and(inner, jnp.logical_and(early >= 0, early < PIECES)))
         def _():
@@ -279,7 +286,7 @@
 
                 wide_to_partner(0, q).start()
 
-        @pl.when(i == 8)
+        @pl.when(i == 7)
         def _():
             for q in range(XPIECES):
                 @pl.when(inner)
@@ -288,7 +295,7 @@
                     wide_to_side(2, 2, q).start()
                     wide_to_partner(2, q).start()
 
-        @pl.when(i == 9)
+        @pl.when(i == 8)
         def _():
             for q in range(XPIECES):
                 wide_to_side(1, 1, q).wait_recv()
@@ -299,14 +306,14 @@
 
                 wide_to_partner(1, q).start()
 
-        @pl.when(jnp.logical_and(i == 14, inner))
+        @pl.when(jnp.logical_and(i == 12, inner))
         def _():
             for q in range(XPIECES):
                 wide_to_across(3, 3, q).wait_recv()
                 wide_to_side(3, 3, q).start()
                 wide_to_partner(3, q).start()
 
-        @pl.when(jnp.logical_and(i == 15, end))
+        @pl.when(jnp.logical_and(i == 13, end))
         def _():
             for q in range(XPIECES):
                 wide_to_side(2, 2, q).wait_recv()
@@ -319,9 +326,9 @@
                 wide_to_partner(3, q).start()
 
     def sums_of(xx):
-        return [acc[pl.ds((c * NX + xx) * rows, rows), :] for c in range(2)]
-
-    def send_sums(k):
+        return [acc[pl.ds((c * NX + xx) * few, few), :] for c in range(2)]
+
+    def send_sums(k, h):
         zz = held_z(k)
         b = lax.rem(zz, 2)
 
@@ -332,37 +339,40 @@
 
                 @pl.when(dy == y)
                 def _():
-                    for h in range(2):
-                        for c, value in enumerate(sums_of(2 * h + t)):
-                            mine[b, h, pl.ds(c * rows, rows), :] = value
+                    for u in range(2):
+                        for c, value in enumerate(sums_of(2 * u + t)):
+                            mine[b, h, u, pl.ds(c * few, few), :] = value
 
                 @pl.when(dy != y)
                 def _():
-                    for h in range(2):
-                        for c, value in enumerate(sums_of(2 * h + t)):
-                            stage_y[k, t, h, pl.ds(c * rows, rows), :] = value.astype(jnp.bfloat16)
-                    to_y(k, t, b, dy).start()
+                    for u in range(2):
+                        for c, value in enumerate(sums_of(2 * u + t)):
+                            stage_y[k, h, t, u, pl.ds(c * few, few), :] = value.astype(jnp.bfloat16)
+                    to_y(k, h, t, b, dy).start()
 
         @pl.when(k == NZ - 1)
         def _():
-            for xx in range(NX):
+            for n in range(NX):
+                xx = lax.rem(n + 2 * (1 - zh), NX)
                 owner = 2 * xx + zz // 2
+                pieces = [acc[pl.ds(pl.multiple_of((c * NX + xx) * few, few), few), :] for c in range(2)]
 
                 @pl.when(owner == g)
                 def _():
-                    for c, value in enumerate(sums_of(xx)):
-                        mine[b, zh, pl.ds(c * rows, rows), :] = value
+                    for c, value in enumerate(pieces):
+                        mine[b, h, zh, pl.ds(c * few, few), :] = value
 
                 @pl.when(owner != g)
                 def _():
-                    for c, value in enumerate(sums_of(xx)):
-                        stage_d[xx, pl.ds(c * rows, rows), :] = value.astype(jnp.bfloat16)
-                    to_owner(xx, owner).start()
+                    for c, value in enumerate(pieces):
+                        stage_d[h, xx, pl.ds(c * few, few), :] = value.astype(jnp.bfloat16)
+                    to_owner(h, xx, owner).start()
 
     def reduce_y(i):
-        k = (i - AT_SUM) // PIECES
-
-        @pl.when(jnp.logical_and(i >= AT_SUM, jnp.logical_and(lax.rem(i - AT_SUM + NZ * PIECES, PIECES) == 0, k < NZ - 1)))
+        n = i - AT_SUM
+        k, h = n // PIECES, lax.rem(n + PIECES, PIECES) // layers
+
+        @pl.when(jnp.logical_and(n >= 0, jnp.logical_and(lax.rem(n + PIECES, layers) == 0, k < NZ - 1)))
         def _():
             zz = held_z(k)
             b = lax.rem(zz, 2)
@@ -370,17 +380,17 @@
             @pl.when(zz // 2 == lax.rem(y, 2))
             def _():
                 for j in range(1, NY):
-                    from_y(b, lax.rem(y + j, NY)).wait_recv()
-
-                def total(h):
-                    value = mine[b, h]
+                    from_y(b, h, lax.rem(y + j, NY)).wait_recv()
+
+                def total(u):
+                    value = mine[b, h, u]
                     for j in range(1, NY):
-                        value = value + landed_y[b, lax.rem(y + j, NY), h].astype(jnp.float32)
+                        value = value + landed_y[b, h, lax.rem(y + j, NY), u].astype(jnp.float32)
                     return value
 
-                stage_z[b] = total(1 - zh).astype(jnp.bfloat16)
-                to_z(b).start()
-                mine[b, zh] = total(zh)
+                stage_z[b, h] = total(1 - zh).astype(jnp.bfloat16)
+                to_z(b, h).start()
+                mine[b, h, zh] = total(zh)
 
     def step(i, carry):
         along_z(i)
@@ -419,38 +429,44 @@
             s = i - AT_D
             k, p = s // PIECES, lax.rem(s, PIECES)
 
+            h, layer = p // layers, lax.rem(p, layers)
+
             def product(lhs, rhs):
-                return lax.dot_general(lhs.reshape(2 * NX * rows, lhs.shape[-1]), rhs, (((1,), (1,)), ((), ())),
+                return lax.dot_general(lhs.reshape(2 * NX * few, lhs.shape[-1]), rhs, (((1,), (1,)), ((), ())),
                                        preferred_element_type=jnp.float32)
 
-            @pl.when(p == 0)
+            @pl.when(s == 0)
             def _():
                 for q in range(XPIECES):
-                    @pl.when(k == 0)
+                    trainx_copy(q).wait()
+
+            @pl.when(s < layers)
+            def _():
+                pltpu.make_async_copy(train.at[layer], train.at[layer], train_sem.at[layer]).wait()
+
+            to_partner(k, p).wait_recv()
+            term = product(held[held_z(k), p], train[layer])
+
+            @pl.when(layer == 0)
+            def _():
+                acc[...] = term
+
+            @pl.when(layer > 0)
+            def _():
+                acc[...] += term
+
+            @pl.when(jnp.logical_or(p == layers - 1, p == layers))
+            def _():
+                for q in range(XPIECES):
+                    @pl.when(h == 0)
                     def _():
-                        trainx_copy(q).wait()
-
-            @pl.when(k == 0)
-            def _():
-                pltpu.make_async_copy(train.at[p], train.at[p], train_sem.at[p]).wait()
-
-            to_partner(k, p).wait_recv()
-            term = product(held[held_z(k), p], train[p])
-
-            @pl.when(p == 0)
-            def _():
-                acc[...] = term
-
-            @pl.when(p > 0)
-            def _():
-                acc[...] += term
-
-            @pl.when(p == PIECES - 1)
-            def _():
-                for q in range(XPIECES):
-                    wide_to_partner(k, q).wait_recv()
-                    acc[...] += product(heldx[held_z(k), q], trainx[q])
-                send_sums(k)
+                        wide_to_partner(k, q).wait_recv()
+
+                    acc[...] += product(heldx[held_z(k), q, :, :, pl.ds(pl.multiple_of(h * few, few), few), :], trainx[q])
+
+            @pl.when(layer == layers - 1)
+            def _():
+                send_sums(k, h)
 
         reduce_y(i)
         return carry
@@ -459,23 +475,27 @@
 
     late_owner = lax.rem(y, 2) != upper
     last_b = lax.rem(held_z(NZ - 1), 2)
-    block = 2 * rows
-    for b in range(2):
-        direct = jnp.logical_and(late_owner, last_b == b)
-        place = pl.ds(b * block, block)
-
-        @pl.when(jnp.logical_not(direct))
-        def _():
-            to_z(b).wait_recv()
-            out_ref[place, :] = mine[b, zh] + landed_z[b].astype(jnp.float32)
-
-        @pl.when(direct)
-        def _():
-            out_ref[place, :] = mine[b, zh]
-            for j in range(1, NG):
-                src = lax.rem(g + j, NG)
-                from_member(src).wait_recv()
-                out_ref[place, :] += landed_d[src].astype(jnp.float32)
+    for h in range(HALVES):
+        for b in range(2):
+            direct = jnp.logical_and(late_owner, last_b == b)
+
+            def put(value):
+                for c in range(2):
+                    out_ref[pl.ds(b * 2 * rows + c * rows + h * few, few), :] = value[c * few:(c + 1) * few]
+
+            @pl.when(jnp.logical_not(direct))
+            def _():
+                to_z(b, h).wait_recv()
+                put(mine[b, h, zh] + landed_z[b, h].astype(jnp.float32))
+
+            @pl.when(direct)
+            def _():
+                value = mine[b, h, zh]
+                for j in range(1, NG):
+                    src = lax.rem(g + j, NG)
+                    from_member(h, src).wait_recv()
+                    value = value + landed_d[h, src].astype(jnp.float32)
+                put(value)
 
     def drain(s, carry):
         k, p = s // PIECES, lax.rem(s, PIECES)
@@ -520,35 +540,37 @@
             wide_to_side(2, 2, q).wait_send()
             wide_to_side(3, 3, q).wait_send()
 
-    for k in range(NZ - 1):
-        zz = held_z(k)
-        for t in range(2):
-            @pl.when(2 * t + zz // 2 != y)
-            def _():
-                to_y(k, t, 0, 0).wait_send()
-
-    for b in range(2):
-        @pl.when(jnp.logical_not(jnp.logical_and(late_owner, last_b == b)))
-        def _():
-            to_z(b).wait_send()
-
-    for xx in range(NX):
-        @pl.when(2 * xx + held_z(NZ - 1) // 2 != g)
-        def _():
-            to_owner(xx, 0).wait_send()
+    for h in range(HALVES):
+        for k in range(NZ - 1):
+            zz = held_z(k)
+            for t in range(2):
+                @pl.when(2 * t + zz // 2 != y)
+                def _():
+                    to_y(k, h, t, 0, 0).wait_send()
+
+        for b in range(2):
+            @pl.when(jnp.logical_not(jnp.logical_and(late_owner, last_b == b)))
+            def _():
+                to_z(b, h).wait_send()
+
+        for xx in range(NX):
+            @pl.when(2 * xx + held_z(NZ - 1) // 2 != g)
+            def _():
+                to_owner(h, xx, 0).wait_send()
 
 
 def on_device(query_grads, train_grads, left_inverse, right_inverse):
     layers, rows, feat = query_grads.shape
     proj = left_inverse.shape[1]
     train_rows = train_grads.shape[1]
-    cols = (feat - XCOLS) * layers // PIECES
+    cols = feat - XCOLS
+    few = rows // HALVES
     block = NX * NZ * 2 * rows // NG
     dma = pltpu.SemaphoreType.DMA
     bf16, f32 = jnp.bfloat16, jnp.float32
     return pl.pallas_call(
         kernel,
-        out_shape=jax.ShapeDtypeStruct((block, train_rows), f32),
+        out_shape=pltpu.VMEM((block, train_rows), f32),
         in_specs=[pl.BlockSpec(memory_space=pl.ANY)] * 4,
         out_specs=pl.BlockSpec(memory_space=pltpu.VMEM),
         scratch_shapes=[
@@ -557,26 +579,27 @@
             pltpu.VMEM((layers, proj, proj), f32),
             pltpu.VMEM((rows * proj // 2, 2 * proj), f32),
             pltpu.VMEM((rows * proj // 2, 2 * proj), f32),
-            pltpu.VMEM((NZ, PIECES, 2, NX, rows, cols), bf16),
+            pltpu.VMEM((NZ, PIECES, 2, NX, few, cols), bf16),
             pltpu.VMEM((NZ, XPIECES, 2, NX, rows, XCOLS), bf16),
-            pltpu.VMEM((PIECES, train_rows, cols), bf16),
+            pltpu.VMEM((layers, train_rows, cols), bf16),
             pltpu.VMEM((XPIECES, train_rows, XCOLS), bf16),
-            pltpu.VMEM((2 * NX * rows, train_rows), f32),
-            pltpu.VMEM((2, 2, 2 * rows, train_rows), f32),
-            pltpu.VMEM((NZ - 1, 2, 2, 2 * rows, train_rows), bf16),
-            pltpu.VMEM((2, NY, 2, 2 * rows, train_rows), bf16),
-            pltpu.VMEM((2, 2 * rows, train_rows), bf16),
-            pltpu.VMEM((2, 2 * rows, train_rows), bf16),
-            pltpu.VMEM((NX, 2 * rows, train_rows), bf16),
-            pltpu.VMEM((NG, 2 * rows, train_rows), bf16),
-            dma((3,)), dma((PIECES,)), dma((XPIECES,)),
+            pltpu.VMEM((2 * NX * few, train_rows), f32),
+            pltpu.VMEM((2, HALVES, 2, 2 * few, train_rows), f32),
+            pltpu.VMEM((NZ - 1, HALVES, 2, 2, 2 * few, train_rows), bf16),
+            pltpu.VMEM((2, HALVES, NY, 2, 2 * few, train_rows), bf16),
+            pltpu.VMEM((2, HALVES, 2 * few, train_rows), bf16),
+            pltpu.VMEM((2, HALVES, 2 * few, train_rows), bf16),
+            pltpu.VMEM((HALVES, NX, 2 * few, train_rows), bf16),
+            pltpu.VMEM((HALVES, NG, 2 * few, train_rows), bf16),
+            dma((3,)), dma((layers,)), dma((XPIECES,)),
             dma((NZ, PIECES)), dma((NZ, PIECES)), dma((NZ, PIECES)),
             dma((2, NZ, PIECES)), dma((2, NZ, PIECES)), dma((2, NZ, PIECES)), dma((2, NZ, PIECES)),
             dma((NZ, PIECES)), dma((NZ, PIECES)),
             dma((NZ, XPIECES)), dma((NZ, XPIECES)), dma((NZ, XPIECES)),
             dma((2, XPIECES)), dma((2, XPIECES)), dma((2, XPIECES)), dma((2, XPIECES)),
             dma((NZ, XPIECES)), dma((NZ, XPIECES)),
-            dma((NZ - 1, 2)), dma((2, NY)), dma((2,)), dma((2,)), dma((NX,)), dma((NG,)),
+            dma((NZ - 1, HALVES, 2)), dma((2, HALVES, NY)), dma((2, HALVES)), dma((2, HALVES)),
+            dma((HALVES, NX)), dma((HALVES, NG)),
         ],
         compiler_params=pltpu.CompilerParams(
             collective_id=0, has_side_effects=True, vmem_limit_bytes=60 * 1024 * 1024),

time: 91.4 us -> 88.4 us (0.967)
  Pallas kernels: 89.4 us -> 87.6 us
  local copies, waits for them, and re-layouts: 1.67 us -> 0.71 us
    pallas_call x1, Pallas kernels: 89.4 us -> 87.6 us  [on_device(): pl.pallas_call(kernel, out_shape=pltpu.VMEM((block, train_rows), f32), in...]
    unnamed x1, local copies, waits for them, and re-layouts: 1.67 us -> 0.71 us
where the time goes in v4:
time: 88.4 us; the launch traced here: 88.3 us
  Pallas kernels  87.6 us (99%)
    pallas_call x1, Pallas kernels, on_device(): pl.pallas_call(kernel, out_shape=pltpu.VMEM((block, train_rows), f32), in...  87.6 us

profile of v4, /device:TPU:24, one launch (start us, length us, event | category | flops | bytes accessed | tf_op | source)
XLA Modules:
  0.0 88.3 jit_solution(9123631041612859322)
XLA Ops:
  0.0 87.6 %shard_map.46 = f32[128,512]{1,0:T(8,128)S(1)} custom-call(bf16[2,32,4096]{2,1,0:T(8,128)(2,1)} %query_ref.1, f32[2,64,64]{2,1,0:T(8,128)} %left_ref.1, f32[2,64,64]{2,1,0:T(8,128)} %right_ref.1, bf16[2,512,4096]{2,1,0:T(8,128)(2,1)} %train_ref.1), custom_call_target="tpu_custom_call" | custom-call | tf_op jit(solution)/shard_map/pallas_call | solution.py:571
  87.6 0.7 copy.6

commit v5 on v4

--- a/solution.py
+++ b/solution.py
@@ -473,30 +473,6 @@
 
     lax.fori_loop(0, STEPS + AT_D, step, 0)
 
-    late_owner = lax.rem(y, 2) != upper
-    last_b = lax.rem(held_z(NZ - 1), 2)
-    for h in range(HALVES):
-        for b in range(2):
-            direct = jnp.logical_and(late_owner, last_b == b)
-
-            def put(value):
-                for c in range(2):
-                    out_ref[pl.ds(b * 2 * rows + c * rows + h * few, few), :] = value[c * few:(c + 1) * few]
-
-            @pl.when(jnp.logical_not(direct))
-            def _():
-                to_z(b, h).wait_recv()
-                put(mine[b, h, zh] + landed_z[b, h].astype(jnp.float32))
-
-            @pl.when(direct)
-            def _():
-                value = mine[b, h, zh]
-                for j in range(1, NG):
-                    src = lax.rem(g + j, NG)
-                    from_member(h, src).wait_recv()
-                    value = value + landed_d[h, src].astype(jnp.float32)
-                put(value)
-
     def drain(s, carry):
         k, p = s // PIECES, lax.rem(s, PIECES)
         for d in range(2):
@@ -548,6 +524,31 @@
                 def _():
                     to_y(k, h, t, 0, 0).wait_send()
 
+    late_owner = lax.rem(y, 2) != upper
+    last_b = lax.rem(held_z(NZ - 1), 2)
+    for h in range(HALVES):
+        for b in range(2):
+            direct = jnp.logical_and(late_owner, last_b == b)
+
+            def put(value):
+                for c in range(2):
+                    out_ref[pl.ds(b * 2 * rows + c * rows + h * few, few), :] = value[c * few:(c + 1) * few]
+
+            @pl.when(jnp.logical_not(direct))
+            def _():
+                to_z(b, h).wait_recv()
+                put(mine[b, h, zh] + landed_z[b, h].astype(jnp.float32))
+
+            @pl.when(direct)
+            def _():
+                value = mine[b, h, zh]
+                for j in range(1, NG):
+                    src = lax.rem(g + j, NG)
+                    from_member(h, src).wait_recv()
+                    value = value + landed_d[h, src].astype(jnp.float32)
+                put(value)
+
+    for h in range(HALVES):
         for b in range(2):
             @pl.when(jnp.logical_not(jnp.logical_and(late_owner, last_b == b)))
             def _():

time: 88.4 us -> 87.9 us (level)
  no operation moved by 1% of the time
where the time goes in v5:
time: 87.9 us; the launch traced here: 87.8 us
  Pallas kernels  87.1 us (99%)
    pallas_call x1, Pallas kernels, on_device(): pl.pallas_call(kernel, out_shape=pltpu.VMEM((block, train_rows), f32), in...  87.1 us

profile of v5, /device:TPU:24, one launch (start us, length us, event | category | flops | bytes accessed | tf_op | source)
XLA Modules:
  0.0 87.8 jit_solution(16353253504196555545)
XLA Ops:
  0.0 87.1 %shard_map.46 = f32[128,512]{1,0:T(8,128)S(1)} custom-call(bf16[2,32,4096]{2,1,0:T(8,128)(2,1)} %query_ref.1, f32[2,64,64]{2,1,0:T(8,128)} %left_ref.1, f32[2,64,64]{2,1,0:T(8,128)} %right_ref.1, bf16[2,512,4096]{2,1,0:T(8,128)(2,1)} %train_ref.1), custom_call_target="tpu_custom_call" | custom-call | tf_op jit(solution)/shard_map/pallas_call | solution.py:572
  87.1 0.7 copy.6

commit v6 on v5

--- a/solution.py
+++ b/solution.py
@@ -125,23 +125,25 @@
 
     for copy in in_copies():
         copy.start()
-    for p in range(layers):
-        train_copy(p).start()
-    for q in range(XPIECES):
-        trainx_copy(q).start()
 
     barrier = pltpu.get_barrier_semaphore()
 
     def greet(target):
         pl.semaphore_signal(barrier, inc=1, device_id=target, device_id_type=MESH)
 
+    for other in (1 - zh, zh):
+        for j in (2, 1, 3, 0):
+            if other is not zh or j > 0:
+                greet((other * NY + lax.rem(y + j, NY), row))
     greet(device(right, z, core))
     greet(device(left, z, core))
     greet(device(x, z, 1 - core))
     greet(device(x, side, core))
     greet(device(x, across, core))
-    for j in range(1, NG):
-        greet((lax.rem(g + j, NG), row))
+    for p in range(layers):
+        train_copy(p).start()
+    for q in range(XPIECES):
+        trainx_copy(q).start()
 
     for copy in in_copies():
         copy.wait()

time: 87.9 us -> 87.4 us (level)
  no operation moved by 1% of the time
where the time goes in v6:
time: 87.4 us; the launch traced here: 87.1 us
  Pallas kernels  86.4 us (99%)
    pallas_call x1, Pallas kernels, on_device(): pl.pallas_call(kernel, out_shape=pltpu.VMEM((block, train_rows), f32), in...  86.4 us

profile of v6, /device:TPU:24, one launch (start us, length us, event | category | flops | bytes accessed | tf_op | source)
XLA Modules:
  0.0 87.1 jit_solution(14434663254509758785)
XLA Ops:
  0.0 86.4 %shard_map.46 = f32[128,512]{1,0:T(8,128)S(1)} custom-call(bf16[2,32,4096]{2,1,0:T(8,128)(2,1)} %query_ref.1, f32[2,64,64]{2,1,0:T(8,128)} %left_ref.1, f32[2,64,64]{2,1,0:T(8,128)} %right_ref.1, bf16[2,512,4096]{2,1,0:T(8,128)(2,1)} %train_ref.1), custom_call_target="tpu_custom_call" | custom-call | tf_op jit(solution)/shard_map/pallas_call | solution.py:574
  86.4 0.7 copy.6
